TPU v7x, 32 devices: a whole 2x2x4 slice. The times are simulated.
32 devices in a mesh: energy: 4 (over z), wire: 8 (over y, x, core).
Axes of the slice: x: 2, y: 2, z: 4, core: 2. Of those that a mesh axis runs over, the one named last changes fastest.
Arguments:
- g_prev: bfloat16 [2, 8, 8, 512, 512], P(None, 'energy', 'wire'), may hold values from -0.25 to 0.25
- local_green: bfloat16 [2, 8, 8, 512, 512], P(None, 'energy', 'wire'), may hold values from -0.09375 to 0.09375
- prop: bfloat16 [2, 8, 8, 512, 512], P(None, 'energy', 'wire'), may hold values from -1.5 to 1.5
- incoming: bfloat16 [2, 8, 8, 64, 512], P(None, 'energy', 'wire'), may hold values from -3 to 3
- plus_partner: int32 [8], replicated, may hold values from -1 to 7
- minus_partner: int32 [8], replicated, may hold values from -1 to 7
- counts: int32 [4], P('energy'), may hold values from 1 to 2
- pot_index: int32 [8], P('wire'), may hold values from 0 to 15
- levels: float32 [16], replicated, may hold values from -1 to 1
- coupling: float32 [2], replicated, may hold values from 0.5 to 2
Outputs:
- scattered: bfloat16 [2, 8, 8, 64, 512], P(None, 'energy', 'wire')
- green_next: bfloat16 [2, 8, 8, 512, 512], P(None, 'energy', 'wire')
Inputs may be any that keep to these rules, and one draw needn't show every extreme that they name: `plus_partner`: -1 means that the partner energy lies outside the window. `minus_partner`: -1 means that the partner energy lies outside the window. The first counts[g] of the 2 slots of group g are live.
All inputs are finite; a program needn't handle non-finite values.
Results may differ from a plain program's by a relative error of at most 0.035.
Values may be sent and summed in bfloat16 or wider, within the bound.
No kernel may reach another device: no remote copies, remote signals or barrier semaphores. Data moves between devices by JAX's collectives and lax.ppermute only.
A program may use at most 192 MiB of HBM per device.

v0:
```python
import jax
import jax.numpy as jnp
from jax import lax
from jax.sharding import PartitionSpec as P


def entering(value, axis, join, neutral):
    count, mine = (lax.axis_size(axis), lax.axis_index(axis))
    pieces = jax.tree.map(lambda part: lax.all_gather(part, axis), value)
    subtotal = jax.tree.map(
        lambda part, zero: jnp.full_like(part, 0) + jnp.asarray(zero, part.dtype), value, neutral
    )

    def step(position, subtotal):
        longer = join(subtotal, jax.tree.map(lambda part: part[position], pieces))
        return jax.tree.map(lambda new, old: jnp.where(position < mine, new, old), longer, subtotal)

    return lax.fori_loop(0, count - 1, step, subtotal)


def complex_product(first_op, second_op):

    def multiply(lhs_part, rhs_part):
        return jnp.einsum("sij,sjk->sik", lhs_part, rhs_part, preferred_element_type=jnp.float32)

    real_part = multiply(first_op[0], second_op[0]) - multiply(first_op[1], second_op[1])
    imag_part = multiply(first_op[0], second_op[1]) + multiply(first_op[1], second_op[0])
    return jnp.stack([real_part, imag_part])


def intersection(first_op, second_op):
    return jnp.einsum("smi,smj->sij", first_op, second_op, preferred_element_type=jnp.float32)


def shards(
    g_prev,
    local_green,
    prop,
    incoming,
    plus_partner,
    minus_partner,
    counts,
    pot_index,
    levels,
    coupling,
):
    slot_count = g_prev.shape[1]
    orbitals = g_prev.shape[3]
    mode_count = incoming.shape[3]
    group_index = lax.axis_index("energy")
    plus_own = lax.dynamic_slice_in_dim(plus_partner, group_index * slot_count, slot_count)
    minus_own = lax.dynamic_slice_in_dim(minus_partner, group_index * slot_count, slot_count)
    incident = incoming[:, :, 0]
    green_here = local_green[:, :, 0]
    steps_here = prop[:, :, 0]
    shard_piece = lax.all_gather(g_prev, "energy", axis=1, tiled=True)
    global_index = jnp.arange(shard_piece.shape[1], dtype=jnp.int32)
    slab_piece = shard_piece[:, :, 0]
    plus_select = (plus_own[:, None] == global_index[None, :]).astype(jnp.bfloat16)
    minus_select = (minus_own[:, None] == global_index[None, :]).astype(jnp.bfloat16)

    def select_rows(selector):
        return jnp.einsum(
            "sk,rkab->rsab", selector, slab_piece, preferred_element_type=jnp.float32
        ).astype(jnp.bfloat16)

    upper_block = select_rows(plus_select)
    lower_block = select_rows(minus_select)
    shifted = coupling[0] * complex_product(incident, upper_block) + coupling[1] * complex_product(
        incident, lower_block
    )
    level_hit = pot_index[0] == jnp.arange(levels.shape[0], dtype=jnp.int32)
    potential = jnp.sum(jnp.where(level_hit, levels, jnp.float32(0.0)))
    source_term = (shifted + potential * incident.astype(jnp.float32)).astype(jnp.bfloat16)
    source = complex_product(source_term, green_here)
    identity = jnp.broadcast_to(
        jnp.eye(orbitals, dtype=jnp.bfloat16), (slot_count, orbitals, orbitals)
    )
    identity_map = jnp.stack([identity, jnp.zeros_like(identity)])
    zero_wave = jnp.zeros((2, slot_count, mode_count, orbitals), jnp.bfloat16)

    def compose(earlier, later):
        step_block = complex_product(earlier[0], later[0]).astype(jnp.bfloat16)
        offset_wave = (complex_product(earlier[1], later[0]) + later[1].astype(jnp.float32)).astype(
            jnp.bfloat16
        )
        return (step_block, offset_wave)

    preceding = entering(
        (steps_here, source.astype(jnp.bfloat16)), "wire", compose, (identity_map, zero_wave)
    )
    chained = (complex_product(preceding[1], steps_here) + source).astype(jnp.bfloat16)
    combined = (incident.astype(jnp.float32) + chained.astype(jnp.float32)).astype(jnp.bfloat16)
    green_real = (
        intersection(combined[1], combined[0]) - intersection(combined[0], combined[1])
    ) / mode_count
    green_imag = (
        intersection(combined[0], combined[0]) + intersection(combined[1], combined[1])
    ) / mode_count
    live_mask = (jnp.arange(slot_count, dtype=jnp.int32) < counts[0])[None, :, None, None]
    scattered = jnp.where(live_mask, chained, jnp.zeros_like(chained))[:, :, None]
    green_block = jnp.stack([green_real, green_imag])
    green_next = jnp.where(live_mask, green_block, jnp.zeros_like(green_block)).astype(
        jnp.bfloat16
    )[:, :, None]
    return (scattered, green_next)


def solution(mesh):
    placed = (
        P(None, "energy", "wire", None, None),
        P(None, "energy", "wire", None, None),
        P(None, "energy", "wire", None, None),
        P(None, "energy", "wire", None, None),
        P(),
        P(),
        P("energy"),
        P("wire"),
        P(),
        P(),
    )
    return jax.shard_map(
        shards,
        mesh=mesh,
        in_specs=placed,
        out_specs=(P(None, "energy", "wire", None, None), P(None, "energy", "wire", None, None)),
        check_vma=False,
    )
```

profile of v0, /device:TPU:0, one launch (start us, length us, event | category | flops | bytes accessed | tf_op | source)
XLA Modules:
  0.0 369.7 jit_solution(1472527370898223248)
XLA Ops:
  7.2 3.0 copy.30
  10.3 0.6 copy-done.8
  11.7 0.6 fusion.77
  12.3 0.7 fusion.74
  13.0 149.8 %all-gather.5.cloned.1.call-done = bf16[2,8,1,512,512]{4,3,2,0,1:T(8,128)(2,1)} async-done(((bf16[2,2,1,512,512]{4,3,2,0,1:T(8,128)(2,1)}), bf16[2,8,1,512,512]{4,3,2,0,1:T(8,128)(2,1)}) %all-gather.5.cloned.1.call-update) | async-done | bytes 8388624 | tf_op jit(solution)/shard_map/all_gather | solution.py:56
  162.8 9.0 %fusion.23 = bf16[2,2,512,512]{3,1,2,0:T(2,128)(2,1)S(1)} fusion(bf16[2,8,1,512,512]{4,3,2,0,1:T(8,128)(2,1)} %all-gather.5.cloned.1.call-done, s32[2]{0:T(128)S(1)} %dynamic_slice.21), kind=kOutput, calls=%fused_computation.28 | convolution fusion | flops 17825808 | bytes 10485768 | tf_op jit(solution)/shard_map/sk,rkab->rsab/dot_general | solution.py:63
  171.8 1.7 slice_bitcast_fusion.11
  173.5 0.3 fusion.41
  173.8 0.3 fusion.39
  174.1 0.3 fusion.31
  174.4 0.3 fusion.30
  174.8 5.2 %fusion.26 = bf16[2,2,512,512]{3,1,2,0:T(2,128)(2,1)S(1)} fusion(bf16[2,8,1,512,512]{4,3,2,0,1:T(8,128)(2,1)S(1)} %bitcast.196, s32[2]{0:T(128)S(1)} %dynamic_slice.20), kind=kOutput, calls=%fused_computation.29 | convolution fusion | flops 17825808 | bytes 10485768 | tf_op jit(solution)/shard_map/sk,rkab->rsab/dot_general | solution.py:63
  180.0 1.5 slice_bitcast_fusion.13
  182.1 0.3 fusion.33
  182.4 0.3 fusion.32
  182.7 2.1 fusion.51
  186.0 0.4 copy-done.3
  186.5 0.7 copy-done.5
  187.1 0.7 pad_maximum_fusion
  187.9 0.7 all-gather.9.cloned.1.call-update
  189.3 24.9 %all-gather.7.cloned.1.call-done = bf16[8,2,2,64,512]{4,3,2,1,0:T(8,128)(2,1)} async-done(((bf16[1,2,2,64,512]{4,3,2,1,0:T(8,128)(2,1)}), bf16[8,2,2,64,512]{4,3,2,1,0:T(8,128)(2,1)}) %all-gather.7.cloned.1.call-update) | async-done | bytes 2097168 | tf_op jit(solution)/shard_map/all_gather | solution.py:9
  214.2 91.8 %all-gather.9.cloned.1.call-done = bf16[16,2,1,512,512]{4,3,2,1,0:T(8,128)(2,1)} async-done(((bf16[2,2,1,512,512]{4,3,2,1,0:T(8,128)(2,1)}), bf16[16,2,1,512,512]{4,3,2,1,0:T(8,128)(2,1)}) %all-gather.9.cloned.1.call-update) | async-done | bytes 16777232 | tf_op jit(solution)/shard_map/all_gather | solution.py:9
  306.0 51.0 %while.14 = (s32[]{:T(128)}, bf16[2,2,64,512]{3,2,1,0:T(8,128)(2,1)S(1)}, s32[]{:T(128)}, bf16[8,2,2,512,512]{4,3,2,1,0:T(8,128)(2,1)}, bf16[8,2,2,64,512]{4,3,2,1,0:T(8,128)(2,1)}, /*index=5*/s32[]{:T(128)}, s32[]{:T(128)}, s32[]{}) while((s32[]{:T(128)}, bf16[2,2,64,512]{3,2,1,0:T(8,128)(2,1)S(1)}, s32[]{:T(128)}, ...), condition=%wide.region_2.3_spmd.clone, body=%wide.region_1.2_spmd.clone.sunk | while | flops 269484032 | bytes 8128642 | solution.py:18
  306.0 1.7 fusion.85
  307.7 1.5 fusion.86
  309.2 1.5 fusion.83
  310.7 1.5 fusion.84
  312.3 1.1 fusion.87
  313.4 1.5 fusion.85
  314.9 1.5 fusion.86
  316.5 1.5 fusion.83
  318.0 1.5 fusion.84
  319.5 1.1 fusion.87
  320.7 1.5 fusion.85
  322.2 1.5 fusion.86
  323.7 1.5 fusion.83
  325.2 1.5 fusion.84
  326.8 1.1 fusion.87
  327.9 1.5 fusion.85
  329.5 1.5 fusion.86
  331.0 1.5 fusion.83
  332.5 1.5 fusion.84
  334.0 1.1 fusion.87
  335.2 1.5 fusion.85
  336.7 1.5 fusion.86
  338.2 1.5 fusion.83
  339.8 1.5 fusion.84
  341.3 1.1 fusion.87
  342.5 1.5 fusion.85
  344.0 1.5 fusion.86
  345.5 1.5 fusion.83
  347.0 1.5 fusion.84
  348.6 1.1 fusion.87
  349.7 1.5 fusion.85
  351.2 1.5 fusion.86
  352.8 1.5 fusion.83
  354.3 1.5 fusion.84
  355.8 1.1 fusion.87
  358.4 0.5 fusion.66
  358.9 0.5 fusion.67
  359.4 0.5 multiply_bitcast_fusion.1
  359.9 0.5 multiply_bitcast_fusion
  360.4 2.0 fusion.29
  362.3 0.8 fusion.57
  (52 shorter events, 3.8 us)
Async XLA Ops:
  7.2 155.6 %all-gather.5.cloned.1.call-start = ((), (), s32[]{:S(2)}) async-start(), calls=%async_computation | async-start | bytes 10485760 | tf_op jit(solution)/shard_map/all_gather | solution.py:56
  10.3 0.7 copy-start.8
  10.3 0.7 copy-start.9
  10.3 1.5 copy-start.7
  10.3 2.1 copy-start.10
  10.3 203.9 %all-gather.7.cloned.1.call-start = ((), (), s32[]{:S(2)}) async-start(), calls=%async_computation.1 | async-start | bytes 2359296 | tf_op jit(solution)/shard_map/all_gather | solution.py:9
  162.8 10.7 %copy-start.1 = (bf16[2,2,1,64,512]{4,3,2,1,0:T(8,128)(2,1)S(1)}, bf16[2,2,1,64,512]{4,3,2,1,0:T(8,128)(2,1)}, u32[]{:S(2)}) copy-start(bf16[2,2,1,64,512]{4,3,2,1,0:T(8,128)(2,1)} %param.15) | copy-start | bytes 786436
  162.8 12.0 %slice-start = ((s8[8388608]{0:T(1024)(128)(4,1)}), s8[4194304]{0:T(1024)(128)(4,1)S(1)}, s32[]{:S(2)}) async-start(s8[8388608]{0:T(1024)(128)(4,1)} %bitcast.195), calls=%async_computation.3 | async-start | bytes 8388608
  171.8 2.9 slice-start.1
  182.1 2.8 copy-start.2
  185.7 0.7 copy-start.3
  186.4 0.7 copy-start.5
  187.9 118.1 %all-gather.9.cloned.1.call-start = ((), (), s32[]{:S(2)}) async-start(), calls=%async_computation.2 | async-start | bytes 18874368 | tf_op jit(solution)/shard_map/all_gather | solution.py:9
  306.0 51.0 %copy-start = (bf16[2,2,1,512,512]{4,3,2,1,0:T(8,128)(2,1)S(1)}, bf16[2,2,1,512,512]{4,3,2,1,0:T(8,128)(2,1)}, u32[]{:S(2)}) copy-start(bf16[2,2,1,512,512]{4,3,2,1,0:T(8,128)(2,1)} %param.14) | copy-start | bytes 6291460
  357.2 1.0 copy-start.4
  357.3 1.0 copy-start.6
Sparse Core Ops, SparseCore 0:
  10.4 152.3 all-gather.4
  188.0 26.1 all-gather.6
  216.1 89.8 all-gather.8
where the time goes:
time: 371 us; the launch traced here: 370 us
  waiting for transfers between devices  267 us (72%)
  matrix products  63.7 us (17%)
  between operations  15.3 us (4%)
  other arithmetic  14.3 us (4%)
  local copies, waits for them, and re-layouts  8.73 us (2%)
    all_gather x1, waiting for transfers between devices, shards(): shard_piece = lax.all_gather(g_prev, 'energy', axis=1, tiled=True)  150 us
    all_gather x2, waiting for transfers between devices, entering(): pieces = jax.tree.map(lambda part: lax.all_gather(part, axis), value)  117 us
    dot_general x44, matrix products, multiply(): jnp.einsum('sij,sjk->sik', lhs_part, rhs_part, preferred_element_type=jnp...  47.6 us
    dot_general x2, matrix products, select_rows(): jnp.einsum('sk,rkab->rsab', selector, slab_piece, preferred_element_type=...  14.2 us
    select_n x7, other arithmetic, step(): jnp.where(position < mine, new, old)  7.62 us
  transfers between devices with their start and end apart: 3, of which 3 were waited for; matrix products, arithmetic and copies ran while one was open for 0% of the time, Pallas kernels for 0%

commit v1 on v0

--- a/solution.py
+++ b/solution.py
@@ -53,7 +53,24 @@
     incident = incoming[:, :, 0]
     green_here = local_green[:, :, 0]
     steps_here = prop[:, :, 0]
-    shard_piece = lax.all_gather(g_prev, "energy", axis=1, tiled=True)
+    size, place, rows = (lax.axis_size("energy"), lax.axis_index("energy"), g_prev.shape[1])
+    right = [(i, (i + 1) % size) for i in range(size)]
+    left = [(i, (i - 1) % size) for i in range(size)]
+    filled = jnp.zeros((*g_prev.shape[:1], size * rows, *g_prev.shape[1 + 1 :]), g_prev.dtype)
+    filled = lax.dynamic_update_slice_in_dim(filled, g_prev, place * rows, axis=1)
+    from_left = from_right = g_prev
+    half = size // 2
+    for step_2 in range(1, half + 1):
+        from_left = lax.ppermute(from_left, "energy", right)
+        filled = lax.dynamic_update_slice_in_dim(
+            filled, from_left, (place - step_2) % size * rows, axis=1
+        )
+        if step_2 < size - half:
+            from_right = lax.ppermute(from_right, "energy", left)
+            filled = lax.dynamic_update_slice_in_dim(
+                filled, from_right, (place + step_2) % size * rows, axis=1
+            )
+    shard_piece = filled
     global_index = jnp.arange(shard_piece.shape[1], dtype=jnp.int32)
     slab_piece = shard_piece[:, :, 0]
     plus_select = (plus_own[:, None] == global_index[None, :]).astype(jnp.bfloat16)

time: 371 us -> 354 us (0.954)
  waiting for transfers between devices: 267 us -> 235 us
  local copies, waits for them, and re-layouts: 8.73 us -> 26.7 us
  matrix products: 63.7 us -> 54.3 us
  starting transfers between devices: 0.12 us -> 5.25 us
    all_gather x1 -> x0, waiting for transfers between devices: 150 us -> none  [shards(): shard_piece = lax.all_gather(g_prev, 'energy', axis=1, tiled=True)]
    ppermute x0 -> x3, waiting for transfers between devices: none -> 117 us  [the longest x2 86.8 us: shards(): from_left = lax.ppermute(from_left, 'energy', right)]
    dynamic_update_slice x0 -> x4, local copies, waits for them, and re-layouts: none -> 17.8 us  [the longest x2 8.83 us: shards(): lax.dynamic_update_slice_in_dim(filled, from_left, (place - step_2) % siz...]
    dot_general x2, matrix products: 14.2 us -> 4.77 us  [select_rows(): jnp.einsum('sk,rkab->rsab', selector, slab_piece, preferred_element_type=...]
    ppermute x0 -> x3, starting transfers between devices: none -> 5.17 us  [the longest x2 3.08 us: shards(): from_left = lax.ppermute(from_left, 'energy', right)]
  transfers between devices with their start and end apart: 3 -> 5, of which waited for: 3 -> 5; matrix products, arithmetic and copies ran while one was open for 0% -> 5% of each run, Pallas kernels for 0% -> 0%
where the time goes in v1:
time: 354 us; the launch traced here: 352 us
  waiting for transfers between devices  235 us (66%)
  matrix products  54.3 us (15%)
  local copies, waits for them, and re-layouts  26.7 us (8%)
  between operations  15.6 us (4%)
  other arithmetic  14.8 us (4%)
  starting transfers between devices  5.25 us (1%)
    all_gather x2, waiting for transfers between devices, entering(): pieces = jax.tree.map(lambda part: lax.all_gather(part, axis), value)  118 us
    ppermute x2, waiting for transfers between devices, shards(): from_left = lax.ppermute(from_left, 'energy', right)  86.8 us
    dot_general x44, matrix products, multiply(): jnp.einsum('sij,sjk->sik', lhs_part, rhs_part, preferred_element_type=jnp...  47.6 us
    ppermute x1, waiting for transfers between devices, shards(): from_right = lax.ppermute(from_right, 'energy', left)  30 us
    dynamic_update_slice x2, local copies, waits for them, and re-layouts, shards(): lax.dynamic_update_slice_in_dim(filled, from_left, (place - step_2) % siz...  8.83 us
    select_n x7, other arithmetic, step(): jnp.where(position < mine, new, old)  7.62 us
  transfers between devices with their start and end apart: 5, of which 5 were waited for; matrix products, arithmetic and copies ran while one was open for 5% of the time, Pallas kernels for 0%

profile of v1, /device:TPU:0, one launch (start us, length us, event | category | flops | bytes accessed | tf_op | source)
XLA Modules:
  0.0 352.2 jit_solution(13773061640856514690)
XLA Ops:
  7.2 3.1 collective-permute-start
  10.3 2.1 collective-permute-start.1
  12.4 46.6 %collective-permute-done = bf16[2,2,1,512,512]{4,3,2,1,0:T(8,128)(2,1)S(1)} collective-permute-done((bf16[2,2,1,512,512]{4,3,2,1,0:T(8,128)(2,1)}, bf16[2,2,1,512,512]{4,3,2,1,0:T(8,128)(2,1)S(1)}, u32[]{:S(2)}, u32[]{:S(2)}) %collective-permute-start) | collective-permute-done | bytes 2097184 | tf_op jit(solution)/shard_map/ppermute | solution.py:64
  59.0 0.7 dynamic_slice.21
  59.8 0.7 dynamic_slice.20
  61.2 1.4 fusion.61
  62.5 1.3 fusion.58
  63.8 0.5 squeeze.140
  64.3 1.0 copy-done.7
  65.4 3.8 %copy_dynamic-update-slice_fusion.3 = bf16[2,8,512,512]{3,1,2,0:T(8,128)(2,1)S(1)} fusion(bf16[2,8,512,512]{3,1,2,0:T(8,128)(2,1)S(1)} %squeeze.140, s32[]{:T(128)S(6)} %select_n.77, bf16[2,2,512,512]{3,2,1,0:T(8,128)(2,1)S(1)} %bitcast.213), kind=kLoop, calls=%fused_computation.28 | loop fusion | bytes 4194308 | tf_op jit(solution)/shard_map/dynamic_update_slice | solution.py:60
  69.2 3.6 %copy_dynamic-update-slice_fusion.2 = bf16[2,8,512,512]{3,1,2,0:T(8,128)(2,1)S(1)} fusion(bf16[2,8,512,512]{3,1,2,0:T(8,128)(2,1)S(1)} %copy_dynamic-update-slice_fusion.3, s32[]{:T(128)S(6)} %select_n.79, bf16[2,2,512,512]{3,2,1,0:T(8,128)(2,1)S(1)} %bitcast.214), kind=kLoop, calls=%fused_computation.27 | loop fusion | bytes 4194308 | tf_op jit(solution)/shard_map/dynamic_update_slice | solution.py:65
  72.8 30.0 %collective-permute-done.1 = bf16[2,2,1,512,512]{4,3,2,1,0:T(8,128)(2,1)} collective-permute-done((bf16[2,2,1,512,512]{4,3,2,1,0:T(8,128)(2,1)}, bf16[2,2,1,512,512]{4,3,2,1,0:T(8,128)(2,1)}, u32[]{:S(2)}, u32[]{:S(2)}) %collective-permute-start.1) | collective-permute-done | bytes 2097184 | tf_op jit(solution)/shard_map/ppermute | solution.py:69
  102.8 5.2 %copy_dynamic-update-slice_fusion.1 = bf16[2,8,512,512]{3,1,2,0:T(8,128)(2,1)S(1)} fusion(bf16[2,8,512,512]{3,1,2,0:T(8,128)(2,1)S(1)} %copy_dynamic-update-slice_fusion.2, s32[]{:T(128)S(6)} %select_n.81, bf16[2,2,512,512]{3,2,1,0:T(8,128)(2,1)} %bitcast.5), kind=kLoop, calls=%fused_computation.26 | loop fusion | bytes 4194308 | tf_op jit(solution)/shard_map/dynamic_update_slice | solution.py:70
  108.1 40.1 %collective-permute-done.2 = bf16[2,2,1,512,512]{4,3,2,1,0:T(8,128)(2,1)} collective-permute-done((bf16[2,2,1,512,512]{4,3,2,1,0:T(8,128)(2,1)S(1)}, bf16[2,2,1,512,512]{4,3,2,1,0:T(8,128)(2,1)}, u32[]{:S(2)}, u32[]{:S(2)}) %collective-permute-start.2) | collective-permute-done | bytes 2097184 | tf_op jit(solution)/shard_map/ppermute | solution.py:64
  148.2 5.2 %copy_dynamic-update-slice_fusion = bf16[2,8,512,512]{3,1,2,0:T(8,128)(2,1)S(1)} fusion(bf16[2,8,512,512]{3,1,2,0:T(8,128)(2,1)S(1)} %copy_dynamic-update-slice_fusion.1, s32[]{:T(128)S(6)} %select_n.83, bf16[2,2,512,512]{3,2,1,0:T(8,128)(2,1)} %bitcast.6), kind=kLoop, calls=%fused_computation.25 | loop fusion | bytes 4194308 | tf_op jit(solution)/shard_map/dynamic_update_slice | solution.py:65
  153.4 2.4 fusion.12
  155.8 1.7 slice_bitcast_fusion.11
  158.8 2.4 fusion.11
  161.1 1.5 slice_bitcast_fusion.13
  163.9 2.1 fusion.35
  167.6 0.7 copy-done.5
  168.3 0.7 pad_maximum_fusion
  169.1 0.7 all-gather.6.cloned.1.call-update
  170.5 26.0 %all-gather.4.cloned.1.call-done = bf16[8,2,2,64,512]{4,3,2,1,0:T(8,128)(2,1)} async-done(((bf16[1,2,2,64,512]{4,3,2,1,0:T(8,128)(2,1)}), bf16[8,2,2,64,512]{4,3,2,1,0:T(8,128)(2,1)}) %all-gather.4.cloned.1.call-update) | async-done | bytes 2097168 | tf_op jit(solution)/shard_map/all_gather | solution.py:9
  196.4 91.8 %all-gather.6.cloned.1.call-done = bf16[16,2,1,512,512]{4,3,2,1,0:T(8,128)(2,1)} async-done(((bf16[2,2,1,512,512]{4,3,2,1,0:T(8,128)(2,1)}), bf16[16,2,1,512,512]{4,3,2,1,0:T(8,128)(2,1)}) %all-gather.6.cloned.1.call-update) | async-done | bytes 16777232 | tf_op jit(solution)/shard_map/all_gather | solution.py:9
  288.2 51.0 %while.14 = (s32[]{:T(128)}, bf16[2,2,64,512]{3,2,1,0:T(8,128)(2,1)S(1)}, s32[]{:T(128)}, bf16[8,2,2,512,512]{4,3,2,1,0:T(8,128)(2,1)}, bf16[8,2,2,64,512]{4,3,2,1,0:T(8,128)(2,1)}, /*index=5*/s32[]{:T(128)}, s32[]{:T(128)}, s32[]{}) while((s32[]{:T(128)}, bf16[2,2,64,512]{3,2,1,0:T(8,128)(2,1)S(1)}, s32[]{:T(128)}, ...), condition=%wide.region_2.3_spmd.clone, body=%wide.region_1.2_spmd.clone.sunk | while | flops 269484032 | bytes 8128642 | solution.py:18
  288.2 1.7 fusion.71
  289.9 1.5 fusion.72
  291.4 1.5 fusion.69
  293.0 1.5 fusion.70
  294.5 1.1 fusion.73
  295.6 1.5 fusion.71
  297.2 1.5 fusion.72
  298.7 1.5 fusion.69
  300.2 1.5 fusion.70
  301.8 1.1 fusion.73
  302.9 1.5 fusion.71
  304.4 1.5 fusion.72
  306.0 1.5 fusion.69
  307.5 1.5 fusion.70
  309.0 1.1 fusion.73
  310.2 1.5 fusion.71
  311.7 1.5 fusion.72
  313.2 1.5 fusion.69
  314.8 1.5 fusion.70
  316.3 1.1 fusion.73
  317.4 1.5 fusion.71
  319.0 1.5 fusion.72
  320.5 1.5 fusion.69
  322.0 1.5 fusion.70
  323.6 1.1 fusion.73
  324.7 1.5 fusion.71
  326.2 1.5 fusion.72
  327.8 1.5 fusion.69
  329.3 1.5 fusion.70
  330.8 1.1 fusion.73
  332.0 1.5 fusion.71
  333.5 1.5 fusion.72
  335.0 1.5 fusion.69
  336.5 1.5 fusion.70
  338.1 1.1 fusion.73
  341.6 0.5 multiply_bitcast_fusion.1
  342.6 2.0 fusion.13
  344.6 0.8 fusion.41
  (48 shorter events, 7.2 us)
Async XLA Ops:
  7.2 189.3 %all-gather.4.cloned.1.call-start = ((), (), s32[]{:S(2)}) async-start(), calls=%async_computation | async-start | bytes 2359296 | tf_op jit(solution)/shard_map/all_gather | solution.py:9
  7.2 51.8 %collective-permute-start = (bf16[2,2,1,512,512]{4,3,2,1,0:T(8,128)(2,1)}, bf16[2,2,1,512,512]{4,3,2,1,0:T(8,128)(2,1)S(1)}, u32[]{:S(2)}, u32[]{:S(2)}) collective-permute-start(bf16[2,2,1,512,512]{4,3,2,1,0:T(8,128)(2,1)} %param.12), channel_id=1, source_target_pairs={{0,8},{8,16},{16,24},{24,0},{1,9},{9,17},{17,25},{25,1},{2,10},{10... | collective-permute-start | bytes 6291464 | tf_op jit(solution)/shard_map/ppermute | solution.py:64
  10.3 92.6 %collective-permute-start.1 = (bf16[2,2,1,512,512]{4,3,2,1,0:T(8,128)(2,1)}, bf16[2,2,1,512,512]{4,3,2,1,0:T(8,128)(2,1)}, u32[]{:S(2)}, u32[]{:S(2)}) collective-permute-start(bf16[2,2,1,512,512]{4,3,2,1,0:T(8,128)(2,1)} %param.12), channel_id=1, source_target_pairs={{0,24},{8,0},{16,8},{24,16},{1,25},{9,1},{17,9},{25,17},{2,26},{10... | collective-permute-start | bytes 6291464 | tf_op jit(solution)/shard_map/ppermute | solution.py:69
  59.0 89.2 %collective-permute-start.2 = (bf16[2,2,1,512,512]{4,3,2,1,0:T(8,128)(2,1)S(1)}, bf16[2,2,1,512,512]{4,3,2,1,0:T(8,128)(2,1)}, u32[]{:S(2)}, u32[]{:S(2)}) collective-permute-start(bf16[2,2,1,512,512]{4,3,2,1,0:T(8,128)(2,1)S(1)} %collective-permute-done), channel_id=1, source_target_pairs={{0,8},{8,16},{16,24},{24,0},{1,9},{9,17},{17,25},{25,1},{2,10},{10... | collective-permute-start | bytes 6291464 | tf_op jit(solution)/shard_map/ppermute | solution.py:64
  63.8 1.6 copy-start.7
  155.8 1.7 copy-start.1
  163.2 2.7 copy-start.2
  166.9 0.7 copy-start.3
  167.6 0.7 copy-start.5
  169.0 119.2 %all-gather.6.cloned.1.call-start = ((), (), s32[]{:S(2)}) async-start(), calls=%async_computation.1 | async-start | bytes 18874368 | tf_op jit(solution)/shard_map/all_gather | solution.py:9
  288.2 51.0 %copy-start = (bf16[2,2,1,512,512]{4,3,2,1,0:T(8,128)(2,1)S(1)}, bf16[2,2,1,512,512]{4,3,2,1,0:T(8,128)(2,1)}, u32[]{:S(2)}) copy-start(bf16[2,2,1,512,512]{4,3,2,1,0:T(8,128)(2,1)} %param.14) | copy-start | bytes 6291460
  339.5 1.0 copy-start.4
  339.5 1.0 copy-start.6
Sparse Core Ops, SparseCore 0:
  169.2 27.2 all-gather.3
  198.3 89.8 all-gather.5
